TPU v7x, 32 devices: a whole 2x2x4 slice. The times are simulated.
32 devices in a mesh: depth: 2 (over y), lat: 8 (over z, x), freq: 2 (over core).
Axes of the slice: x: 2, y: 2, z: 4, core: 2. Of those that a mesh axis runs over, the one named last changes fastest.
Arguments:
- surface: bfloat16 [6, 2, 128, 8192], P('freq', None, None, 'lat'), may hold values from -6 to 6
- refl: float32 [2, 8192], P('depth', 'lat'), may hold values from -0.5 to 0.5
- pool: bfloat16 [2, 6, 8, 128, 256], P('depth', 'freq'), may hold values from -0.375 to 0.375
- tile_ids: int32 [2, 64, 10], P('depth', 'lat'), may hold values from 0 to 63, as said below
- block_ids: int32 [2, 64, 10], P('depth', 'lat'), may hold values from 0 to 7
- counts: int32 [2, 64], P('depth', 'lat'), may hold values from 1 to 10, as said below
Outputs:
- image: float32 [2, 8192], P('depth', 'lat')
Inputs may be any that keep to these rules, and one draw needn't show every extreme that they name: tile_ids[l, j, k] = (j + o) mod 64 for an offset o with -8 <= o <= 8; slot 0 names the row's own tile; in every level some row has all 10 slots live with offsets 8 at slot 1 and -8 at slot 2. Slots k >= counts[l, j] of row j are padding; in every level some row has all 10 slots live.
All inputs are finite; a program needn't handle non-finite values.
Results may differ from a plain program's by a relative error of at most 0.00055.
Values may be sent and summed in bfloat16 or wider, within the bound.
No kernel may reach another device: no remote copies, remote signals or barrier semaphores. Data moves between devices by JAX's collectives and lax.ppermute only.
A program may use at most 128 MiB of HBM per device.

v0:
```python
import jax
import jax.numpy as jnp
from jax import lax
from jax.sharding import PartitionSpec as P

TILE = 128
TILE_DEV = 8


def extended_2(block, sides, width):
    for axis, dim in sides:
        count = lax.axis_size(axis)
        forward = [(i, i + 1) for i in range(count - 1)]
        forward.append((count - 1, 0))
        backward = [(target, source) for source, target in forward]
        low = lax.ppermute(
            lax.slice_in_dim(block, block.shape[dim] - width, None, axis=dim), axis, forward
        )
        high = lax.ppermute(lax.slice_in_dim(block, 0, width, axis=dim), axis, backward)
        block = jnp.concatenate([low, block, high], axis=dim)
    return block


def aperture_rim(wave_field):
    return extended_2(wave_field, (("lat", 3),), TILE_DEV * TILE)


def extrapolate(extended, pool_level, local_ids, block_level, count_level, refl_level):
    freqs_here = extended.shape[0]
    shot_rows = extended.shape[2]
    tile_rows = local_ids.shape[0]
    slot_total = local_ids.shape[1]
    tile_grid = extended.reshape(freqs_here, 2, shot_rows, -1, TILE)
    slot_live = (jnp.arange(slot_total)[None, :] < count_level[:, None]).astype(jnp.bfloat16)
    picked = jnp.take(tile_grid, local_ids, axis=3) * slot_live[None, None, None, :, :, None]
    chosen = jnp.take(pool_level, block_level, axis=1)
    product = jnp.einsum("fsarkt,frktc->rfsac", picked, chosen, preferred_element_type=jnp.float32)
    real_part = product[:, :, 0, :, :TILE] - product[:, :, 1, :, TILE:]
    imag_part = product[:, :, 0, :, TILE:] + product[:, :, 1, :, :TILE]
    row_scale = 1.0 / jnp.sqrt(count_level.astype(jnp.float32))
    rows_out = jnp.stack([real_part, imag_part], 2) * row_scale[:, None, None, None, None]
    wave_out = jnp.transpose(rows_out, (1, 2, 3, 0, 4)).reshape(
        freqs_here, 2, shot_rows, tile_rows * TILE
    )
    wave_out = wave_out * (1.0 - refl_level)
    return (wave_out.astype(jnp.bfloat16), jnp.sum(wave_out * wave_out, axis=(0, 1, 2)))


def per_device(surface, refl, pool, tile_ids, block_ids, counts):
    depth_index = lax.axis_index("depth")
    lat_index = lax.axis_index("lat")
    tile_count = TILE_DEV * lax.axis_size("lat")
    first_tile = lat_index * TILE_DEV - TILE_DEV
    freqs_here = surface.shape[0]
    shot_total = surface.shape[2]
    lateral_width = surface.shape[3]
    shot_rows = shot_total // lax.axis_size("depth")
    own_shots = lax.dynamic_slice_in_dim(surface, depth_index * shot_rows, shot_rows, 2)
    pool_all = lax.all_gather(pool, "depth", axis=0, tiled=True)
    ids_all, blocks_all, counts_all = (
        lax.all_gather(tile_ids, "depth", axis=0, tiled=True),
        lax.all_gather(block_ids, "depth", axis=0, tiled=True),
        lax.all_gather(counts, "depth", axis=0, tiled=True),
    )
    refl_all = lax.all_gather(refl, "depth", axis=0, tiled=True)
    level_total = pool_all.shape[0]

    def level_step(level_index, loop_state):
        wave_field, images = loop_state
        ids_here = lax.dynamic_index_in_dim(ids_all, level_index, 0, keepdims=False)
        local_level = jnp.mod(ids_here - first_tile, tile_count)
        pool_here = lax.dynamic_index_in_dim(pool_all, level_index, 0, keepdims=False)
        blocks_here = lax.dynamic_index_in_dim(blocks_all, level_index, 0, keepdims=False)
        counts_here = lax.dynamic_index_in_dim(counts_all, level_index, 0, keepdims=False)
        refl_here = lax.dynamic_index_in_dim(refl_all, level_index, 0, keepdims=False)
        handed, partial_value = extrapolate(
            aperture_rim(wave_field), pool_here, local_level, blocks_here, counts_here, refl_here
        )
        images = lax.dynamic_update_index_in_dim(images, partial_value, level_index, 0)
        return (handed, images)

    start_images = jnp.zeros((level_total, lateral_width), jnp.float32)
    loop_state = lax.fori_loop(0, level_total, level_step, (own_shots, start_images))
    image_local = lax.psum_scatter(loop_state[1], "depth", scatter_dimension=0, tiled=True)[0]
    summed = lax.psum(image_local, "freq")
    divisor = freqs_here * lax.axis_size("freq") * shot_total
    return (summed / divisor)[None, :]


def solution(mesh):
    placed = (
        P("freq", None, None, "lat"),
        P("depth", "lat"),
        P("depth", "freq", None, None, None),
        P("depth", "lat", None),
        P("depth", "lat", None),
        P("depth", "lat"),
    )
    return jax.shard_map(
        per_device, mesh=mesh, in_specs=placed, out_specs=P("depth", "lat"), check_vma=False
    )
```

profile of v0, /device:TPU:0, one launch (start us, length us, event | category | flops | bytes accessed | tf_op | source)
XLA Modules:
  0.0 194.0 jit_solution(9081155011961694617)
XLA Ops:
  6.5 0.0 copy-start
  6.5 0.0 all-gather.4.cloned.1.call-start
  6.5 0.7 all-gather.4.cloned.1.call-update
  7.3 5.4 %all-gather = s32[2,1,8]{2,1,0:T(1,128)S(1)} all-gather(s32[1,1,8]{2,1,0:T(1,128)} %bitcast.109), channel_id=1, replica_groups=mesh['depth'=2,'lat'=8,'freq'=2] {'depth'}, dimensions={0}, use_global_device_ids=true | all-gather | bytes 96 | tf_op jit(solution)/shard_map/all_gather | solution.py:63
  12.7 4.5 %all-gather.1 = f32[2,1,1024]{2,1,0:T(1,128)S(1)} all-gather(f32[1,1,1024]{2,1,0:T(1,128)} %bitcast.108), channel_id=1, replica_groups=mesh['depth'=2,'lat'=8,'freq'=2] {'depth'}, dimensions={0}, use_global_device_ids=true | all-gather | bytes 12288 | tf_op jit(solution)/shard_map/all_gather | solution.py:65
  17.2 1.2 dynamic-slice
  18.4 4.5 %all_gather.15 = s32[2,8,10]{2,1,0:T(8,128)S(1)} all-gather(s32[1,8,10]{2,1,0:T(8,128)} %param.11), channel_id=1, replica_groups=mesh['depth'=2,'lat'=8,'freq'=2] {'depth'}, dimensions={0}, use_global_device_ids=true | all-gather | bytes 960 | tf_op jit(solution)/shard_map/all_gather | solution.py:61
  22.9 4.8 %all_gather.17 = s32[2,8,10]{2,1,0:T(8,128)S(1)} all-gather(s32[1,8,10]{2,1,0:T(8,128)} %param.12), channel_id=1, replica_groups=mesh['depth'=2,'lat'=8,'freq'=2] {'depth'}, dimensions={0}, use_global_device_ids=true | all-gather | bytes 960 | tf_op jit(solution)/shard_map/all_gather | solution.py:62
  27.7 0.0 copy-done
  27.7 1.0 constant_dynamic-slice_fusion.2
  28.7 28.0 %all-gather.4.cloned.1.call-done = bf16[2,3,8,128,256]{4,3,2,1,0:T(8,128)(2,1)} async-done(((bf16[1,3,8,128,256]{4,3,2,1,0:T(8,128)(2,1)}), bf16[2,3,8,128,256]{4,3,2,1,0:T(8,128)(2,1)}) %all-gather.4.cloned.1.call-update) | async-done | bytes 3145744 | tf_op jit(solution)/shard_map/all_gather | solution.py:59
  56.7 121.8 %while.17 = (s32[]{:T(128)}, bf16[3,2,64,1024]{3,2,1,0:T(8,128)(2,1)}, f32[2,1024]{1,0:T(2,128)S(1)}, s32[2,8,10]{2,1,0:T(8,128)S(1)}, s32[]{:T(128)}, /*index=5...) while((s32[]{:T(128)}, ...), condition=%wide.region_2.3_spmd, body=%wide.region_0.2_spmd.sunk | while | flops 2040010240 | bytes 96773536 | solution.py:83
  56.7 4.2 %collective-permute-start = (bf16[3,2,64,1024]{3,2,1,0:T(8,128)(2,1)}, bf16[3,2,64,1024]{3,2,1,0:T(8,128)(2,1)}, u32[]{:S(2)}, u32[]{:S(2)}) collective-permute-start(bf16[3,2,64,1024]{3,2,1,0:T(8,128)(2,1)} %get-tuple-element.336), channel_id=1, source_target_pairs={{2,0},{4,2},{6,4},{8,6},{10,8},{12,10},{14,12},{0,14},{3,1},{5,3},... | collective-permute-start | bytes 2359304 | tf_op jit(solution)/shard_map/while/body/eval_jaxpr/ppermute | solution.py:19
  60.9 0.0 collective-permute-start.1
  60.9 1.5 dynamic-slice_bitcast_fusion.2
  62.5 0.1 reshape.235
  62.5 0.1 reshape.236
  62.6 8.2 %gather_fusion = bf16[80,3,128,256]{3,2,1,0:T(8,128)(2,1)} fusion(bf16[3,8,128,256]{3,2,1,0:T(8,128)(2,1)S(1)} %dynamic-slice_bitcast_fusion.2, s32[1024]{0:T(1024)S(1)} %pad_clamp_fusion.4), kind=kCustom, calls=%fused_computation.1.clone.1 | custom fusion | bytes 31457600 | tf_op jit(solution)/shard_map/while/body/eval_jaxpr/jit(_take)/gather | solution.py:36
  70.9 0.1 fusion.28
  71.0 22.1 %collective-permute-done = bf16[3,2,64,1024]{3,2,1,0:T(8,128)(2,1)} collective-permute-done((bf16[3,2,64,1024]{3,2,1,0:T(8,128)(2,1)}, bf16[3,2,64,1024]{3,2,1,0:T(8,128)(2,1)}, u32[]{:S(2)}, u32[]{:S(2)}) %collective-permute-start) | collective-permute-done | bytes 786464 | tf_op jit(solution)/shard_map/while/body/eval_jaxpr/ppermute | solution.py:19
  93.1 0.0 collective-permute-done.1
  93.1 3.6 %copy_bitcast_fusion.3 = bf16[3,2,64,24,128]{4,2,3,1,0:T(8,128)(2,1)} fusion(bf16[3,2,64,1024]{3,2,1,0:T(8,128)(2,1)} %collective-permute-done, bf16[3,2,64,1024]{3,2,1,0:T(8,128)(2,1)} %get-tuple-element.336, bf16[3,2,64,1024]{3,2,1,0:T(8,128)(2,1)} %collective-permute-done.1), kind=kLoop, calls=%fused_computation.7.clone.1 | loop fusion | flops 7077888 | bytes 4718592 | tf_op jit(solution)/shard_map/while/body/eval_jaxpr/reshape | solution.py:33
  96.7 8.5 %gather_fusion.1 = bf16[80,3,2,64,128]{4,3,2,1,0:T(8,128)(2,1)} fusion(bf16[3,2,64,24,128]{4,2,3,1,0:T(8,128)(2,1)} %copy_bitcast_fusion.3, s32[1024]{0:T(1024)S(1)} %pad_clamp_fusion.5), kind=kCustom, calls=%fused_computation.clone.1 | custom fusion | bytes 15728960 | tf_op jit(solution)/shard_map/while/body/eval_jaxpr/jit(_take)/gather | solution.py:35
  105.2 10.2 %fusion.29 = f32[8,3,2,64,256]{4,3,2,1,0:T(8,128)S(1)} fusion(bf16[8,10,3,128,256]{4,3,2,1,0:T(8,128)(2,1)} %bitcast.101, pred[8,10]{1,0:T(8,128)(4,1)S(1)} %get-tuple-element.317, bf16[8,10,3,2,64,128]{5,4,3,2,1,0:T(8,128)(2,1)} %bitcast.100, pred[8,10]{1,0:T(8,128)(4,1)S(1)} %get-tuple-element.319, bf16[8,10]{1,0:T(8,128)(2,1)S(1)} %fusion.28), kind=kOutput, calls=%fused_computation.9.clone.1 | convolution fusion | flops 2028994560 | bytes 26739008 | tf_op jit(solution)/shard_map/while/body/eval_jaxpr/fsarkt,frktc->rfsac/dot_general | solution.py:37
  115.5 0.2 slice_subtract_fusion.2
  115.7 0.3 fusion.31
  116.0 1.2 fusion.30
  117.2 4.5 %collective-permute-start = (bf16[3,2,64,1024]{3,2,1,0:T(8,128)(2,1)}, bf16[3,2,64,1024]{3,2,1,0:T(8,128)(2,1)}, u32[]{:S(2)}, u32[]{:S(2)}) collective-permute-start(bf16[3,2,64,1024]{3,2,1,0:T(8,128)(2,1)} %get-tuple-element.336), channel_id=1, source_target_pairs={{2,0},{4,2},{6,4},{8,6},{10,8},{12,10},{14,12},{0,14},{3,1},{5,3},... | collective-permute-start | bytes 2359304 | tf_op jit(solution)/shard_map/while/body/eval_jaxpr/ppermute | solution.py:19
  121.7 0.0 collective-permute-start.1
  121.7 1.5 dynamic-slice_bitcast_fusion.2
  123.2 0.1 reshape.235
  123.3 0.1 reshape.236
  123.4 8.2 %gather_fusion = bf16[80,3,128,256]{3,2,1,0:T(8,128)(2,1)} fusion(bf16[3,8,128,256]{3,2,1,0:T(8,128)(2,1)S(1)} %dynamic-slice_bitcast_fusion.2, s32[1024]{0:T(1024)S(1)} %pad_clamp_fusion.4), kind=kCustom, calls=%fused_computation.1.clone.1 | custom fusion | bytes 31457600 | tf_op jit(solution)/shard_map/while/body/eval_jaxpr/jit(_take)/gather | solution.py:36
  131.6 0.1 fusion.28
  131.7 22.7 %collective-permute-done = bf16[3,2,64,1024]{3,2,1,0:T(8,128)(2,1)} collective-permute-done((bf16[3,2,64,1024]{3,2,1,0:T(8,128)(2,1)}, bf16[3,2,64,1024]{3,2,1,0:T(8,128)(2,1)}, u32[]{:S(2)}, u32[]{:S(2)}) %collective-permute-start) | collective-permute-done | bytes 786464 | tf_op jit(solution)/shard_map/while/body/eval_jaxpr/ppermute | solution.py:19
  154.4 0.0 collective-permute-done.1
  154.4 3.6 %copy_bitcast_fusion.3 = bf16[3,2,64,24,128]{4,2,3,1,0:T(8,128)(2,1)} fusion(bf16[3,2,64,1024]{3,2,1,0:T(8,128)(2,1)} %collective-permute-done, bf16[3,2,64,1024]{3,2,1,0:T(8,128)(2,1)} %get-tuple-element.336, bf16[3,2,64,1024]{3,2,1,0:T(8,128)(2,1)} %collective-permute-done.1), kind=kLoop, calls=%fused_computation.7.clone.1 | loop fusion | flops 7077888 | bytes 4718592 | tf_op jit(solution)/shard_map/while/body/eval_jaxpr/reshape | solution.py:33
  158.0 8.5 %gather_fusion.1 = bf16[80,3,2,64,128]{4,3,2,1,0:T(8,128)(2,1)} fusion(bf16[3,2,64,24,128]{4,2,3,1,0:T(8,128)(2,1)} %copy_bitcast_fusion.3, s32[1024]{0:T(1024)S(1)} %pad_clamp_fusion.5), kind=kCustom, calls=%fused_computation.clone.1 | custom fusion | bytes 15728960 | tf_op jit(solution)/shard_map/while/body/eval_jaxpr/jit(_take)/gather | solution.py:35
  166.6 10.2 %fusion.29 = f32[8,3,2,64,256]{4,3,2,1,0:T(8,128)S(1)} fusion(bf16[8,10,3,128,256]{4,3,2,1,0:T(8,128)(2,1)} %bitcast.101, pred[8,10]{1,0:T(8,128)(4,1)S(1)} %get-tuple-element.317, bf16[8,10,3,2,64,128]{5,4,3,2,1,0:T(8,128)(2,1)} %bitcast.100, pred[8,10]{1,0:T(8,128)(4,1)S(1)} %get-tuple-element.319, bf16[8,10]{1,0:T(8,128)(2,1)S(1)} %fusion.28), kind=kOutput, calls=%fused_computation.9.clone.1 | convolution fusion | flops 2028994560 | bytes 26739008 | tf_op jit(solution)/shard_map/while/body/eval_jaxpr/fsarkt,frktc->rfsac/dot_general | solution.py:37
  176.8 0.2 slice_subtract_fusion.2
  177.0 0.3 fusion.31
  177.3 1.2 fusion.30
  178.5 5.0 %all-reduce = f32[2,1024]{1,0:T(2,128)S(1)} all-reduce(f32[2,1024]{1,0:T(2,128)S(1)} %get-tuple-element.226), channel_id=2, replica_groups=mesh['depth'=2,'lat'=8,'freq'=2] {'depth'}, use_global_device_ids=true, to_apply=%region_3.4.clone | all-reduce | flops 2048 | bytes 16384
  183.5 0.6 constant_dynamic-slice_fusion.1
  184.1 2.5 %psum.7 = f32[1024]{0:T(1024)S(1)} all-reduce(f32[1024]{0:T(1024)S(1)} %bitcast.106), channel_id=1, replica_groups=mesh['depth'=2,'lat'=8,'freq'=2] {'freq'}, use_global_device_ids=true, to_apply=%region_4.5 | all-reduce | flops 1024 | bytes 8192 | tf_op jit(solution)/shard_map/psum | solution.py:85
  186.6 0.6 broadcast_multiply_fusion
  (16 shorter events, 0.2 us)
Async XLA Ops:
  6.5 21.1 %copy-start = (bf16[3,2,128,1024]{3,2,1,0:T(8,128)(2,1)S(1)}, bf16[3,2,128,1024]{3,2,1,0:T(8,128)(2,1)}, u32[]{:S(2)}) copy-start(bf16[3,2,128,1024]{3,2,1,0:T(8,128)(2,1)} %param.8) | copy-start | bytes 4718596
  6.5 50.1 %all-gather.4.cloned.1.call-start = ((), (), s32[]{:S(2)}) async-start(), calls=%async_computation | async-start | bytes 4718592 | tf_op jit(solution)/shard_map/all_gather | solution.py:59
  56.7 36.4 %collective-permute-start = (bf16[3,2,64,1024]{3,2,1,0:T(8,128)(2,1)}, bf16[3,2,64,1024]{3,2,1,0:T(8,128)(2,1)}, u32[]{:S(2)}, u32[]{:S(2)}) collective-permute-start(bf16[3,2,64,1024]{3,2,1,0:T(8,128)(2,1)} %get-tuple-element.336), channel_id=1, source_target_pairs={{2,0},{4,2},{6,4},{8,6},{10,8},{12,10},{14,12},{0,14},{3,1},{5,3},... | collective-permute-start | bytes 2359304 | tf_op jit(solution)/shard_map/while/body/eval_jaxpr/ppermute | solution.py:19
  60.9 32.1 %collective-permute-start.1 = (bf16[3,2,64,1024]{3,2,1,0:T(8,128)(2,1)}, bf16[3,2,64,1024]{3,2,1,0:T(8,128)(2,1)}, u32[]{:S(2)}, u32[]{:S(2)}) collective-permute-start(bf16[3,2,64,1024]{3,2,1,0:T(8,128)(2,1)} %get-tuple-element.336), channel_id=1, source_target_pairs={{0,2},{2,4},{4,6},{6,8},{8,10},{10,12},{12,14},{14,0},{1,3},{3,5},... | collective-permute-start | bytes 2359304 | tf_op jit(solution)/shard_map/while/body/eval_jaxpr/ppermute | solution.py:16
  117.2 37.2 %collective-permute-start = (bf16[3,2,64,1024]{3,2,1,0:T(8,128)(2,1)}, bf16[3,2,64,1024]{3,2,1,0:T(8,128)(2,1)}, u32[]{:S(2)}, u32[]{:S(2)}) collective-permute-start(bf16[3,2,64,1024]{3,2,1,0:T(8,128)(2,1)} %get-tuple-element.336), channel_id=1, source_target_pairs={{2,0},{4,2},{6,4},{8,6},{10,8},{12,10},{14,12},{0,14},{3,1},{5,3},... | collective-permute-start | bytes 2359304 | tf_op jit(solution)/shard_map/while/body/eval_jaxpr/ppermute | solution.py:19
  121.7 32.8 %collective-permute-start.1 = (bf16[3,2,64,1024]{3,2,1,0:T(8,128)(2,1)}, bf16[3,2,64,1024]{3,2,1,0:T(8,128)(2,1)}, u32[]{:S(2)}, u32[]{:S(2)}) collective-permute-start(bf16[3,2,64,1024]{3,2,1,0:T(8,128)(2,1)} %get-tuple-element.336), channel_id=1, source_target_pairs={{0,2},{2,4},{4,6},{6,8},{8,10},{10,12},{12,14},{14,0},{1,3},{3,5},... | collective-permute-start | bytes 2359304 | tf_op jit(solution)/shard_map/while/body/eval_jaxpr/ppermute | solution.py:16
Sparse Core Ops, SparseCore 0:
  8.9 47.7 all-gather.3
where the time goes:
time: 194 us
  waiting for transfers between devices  73.5 us (38%)
  local copies, waits for them, and re-layouts  39.6 us (20%)
  blocking collectives  26.7 us (14%)
  matrix products  20.5 us (11%)
  between operations  13.4 us (7%)
  other arithmetic  11.5 us (6%)
  starting transfers between devices  8.71 us (4%)
    ppermute x2, waiting for transfers between devices, extended_2(): lax.ppermute(lax.slice_in_dim(block, 0, width, axis=dim), axis, backward)  44.8 us
    all_gather x1, waiting for transfers between devices, per_device(): pool_all = lax.all_gather(pool, 'depth', axis=0, tiled=True)  28 us
    dot_general x2, matrix products, extrapolate(): jnp.einsum('fsarkt,frktc->rfsac', picked, chosen, preferred_element_type=...  20.5 us
    gather x2, local copies, waits for them, and re-layouts, extrapolate(): jnp.take(tile_grid, local_ids, axis=3)  17 us
    gather x2, local copies, waits for them, and re-layouts, extrapolate(): chosen = jnp.take(pool_level, block_level, axis=1)  16.4 us
    ppermute x2, starting transfers between devices, extended_2(): lax.ppermute(lax.slice_in_dim(block, 0, width, axis=dim), axis, backward)  8.71 us
    reshape x2, other arithmetic, extrapolate(): tile_grid = extended.reshape(freqs_here, 2, shot_rows, -1, TILE)  7.29 us
    all_gather x1, blocking collectives, per_device(): lax.all_gather(counts, 'depth', axis=0, tiled=True)  5.4 us
  transfers between devices with their start and end apart: 5, of which 3 were waited for; matrix products, arithmetic and copies ran while one was open for 11% of the time, Pallas kernels for 0%

commit v1 on v0

--- a/solution.py
+++ b/solution.py
@@ -5,6 +5,24 @@
 
 TILE = 128
 TILE_DEV = 8
+
+
+def laid_out(tiles, dim):
+    shape = list(tiles.shape[1:])
+    shape[dim] *= tiles.shape[0]
+    return jnp.moveaxis(tiles, 0, dim).reshape(shape)
+
+
+def collected_by_bits(array, axis):
+    size = lax.axis_size(axis)
+    pieces = array[None]
+    for level in range(size.bit_length() - 1):
+        bit = 1 << level
+        other = lax.ppermute(pieces, axis, [(i, i ^ bit) for i in range(size)])
+        both = jnp.stack([pieces, other])
+        upper = lax.axis_index(axis) >> level & 1
+        pieces = jnp.where(upper == 0, both, both[::-1]).reshape(-1, *array.shape)
+    return pieces
 
 
 def extended_2(block, sides, width):
@@ -56,7 +74,7 @@
     lateral_width = surface.shape[3]
     shot_rows = shot_total // lax.axis_size("depth")
     own_shots = lax.dynamic_slice_in_dim(surface, depth_index * shot_rows, shot_rows, 2)
-    pool_all = lax.all_gather(pool, "depth", axis=0, tiled=True)
+    pool_all = laid_out(collected_by_bits(pool, "depth"), 0)
     ids_all, blocks_all, counts_all = (
         lax.all_gather(tile_ids, "depth", axis=0, tiled=True),
         lax.all_gather(block_ids, "depth", axis=0, tiled=True),

time: 194 us -> 185 us (0.954)
  waiting for transfers between devices: 73.5 us -> 40 us
  blocking collectives: 26.7 us -> 55.6 us
  between operations: 13.4 us -> 0.03 us
  other arithmetic: 11.5 us -> 15.7 us
  starting transfers between devices: 8.71 us -> 12.5 us
    all_gather x1, blocking collectives: 5.4 us -> 34.7 us  [per_device(): lax.all_gather(counts, 'depth', axis=0, tiled=True)]
    all_gather x1 -> x0, waiting for transfers between devices: 28 us -> none  [per_device(): pool_all = lax.all_gather(pool, 'depth', axis=0, tiled=True)]
    ppermute x2, waiting for transfers between devices: 44.8 us -> 40 us  [extended_2(): lax.ppermute(lax.slice_in_dim(block, 0, width, axis=dim), axis, backward)]
    another operation x0 -> x2, other arithmetic: none -> 4.25 us  [the longest x1 2.56 us: laid_out(): return jnp.moveaxis(tiles, 0, dim).reshape(shape)]
    ppermute x0 -> x1, starting transfers between devices: none -> 3 us  [collected_by_bits(): other = lax.ppermute(pieces, axis, [(i, i ^ bit) for i in range(size)])]
  transfers between devices with their start and end apart: 5 -> 5, of which waited for: 3 -> 2; matrix products, arithmetic and copies ran while one was open for 11% -> 12% of each run, Pallas kernels for 0% -> 0%
where the time goes in v1:
time: 185 us; the launch traced here: 184 us
  blocking collectives  55.6 us (30%)
  waiting for transfers between devices  40 us (22%)
  local copies, waits for them, and re-layouts  39.7 us (21%)
  matrix products  20.5 us (11%)
  other arithmetic  15.7 us (8%)
  starting transfers between devices  12.5 us (7%)
    ppermute x2, waiting for transfers between devices, extended_2(): lax.ppermute(lax.slice_in_dim(block, 0, width, axis=dim), axis, backward)  40 us
    all_gather x1, blocking collectives, per_device(): lax.all_gather(counts, 'depth', axis=0, tiled=True)  34.7 us
    dot_general x2, matrix products, extrapolate(): jnp.einsum('fsarkt,frktc->rfsac', picked, chosen, preferred_element_type=...  20.5 us
    gather x2, local copies, waits for them, and re-layouts, extrapolate(): jnp.take(tile_grid, local_ids, axis=3)  17 us
    gather x2, local copies, waits for them, and re-layouts, extrapolate(): chosen = jnp.take(pool_level, block_level, axis=1)  16.4 us
    ppermute x2, starting transfers between devices, extended_2(): lax.ppermute(lax.slice_in_dim(block, 0, width, axis=dim), axis, backward)  9.53 us
    reshape x2, other arithmetic, extrapolate(): tile_grid = extended.reshape(freqs_here, 2, shot_rows, -1, TILE)  7.31 us
    unnamed x1, blocking collectives  5 us
  transfers between devices with their start and end apart: 5, of which 2 were waited for; matrix products, arithmetic and copies ran while one was open for 12% of the time, Pallas kernels for 0%

profile of v1, /device:TPU:0, one launch (start us, length us, event | category | flops | bytes accessed | tf_op | source)
XLA Modules:
  0.0 184.3 jit_solution(8825564734286021359)
XLA Ops:
  0.0 0.0 copy-start
  0.0 3.0 %collective-permute-start.2 = (bf16[1,1,3,8,128,256]{5,4,3,2,1,0:T(8,128)(2,1)}, bf16[1,1,3,8,128,256]{5,4,3,2,1,0:T(8,128)(2,1)S(1)}, u32[]{:S(2)}, u32[]{:S(2)}) collective-permute-start(bf16[1,1,3,8,128,256]{5,4,3,2,1,0:T(8,128)(2,1)} %bitcast.107), channel_id=1, source_target_pairs={{0,16},{16,0},{1,17},{17,1},{2,18},{18,2},{3,19},{19,3},{4,20},{20... | collective-permute-start | bytes 4718600 | tf_op jit(solution)/shard_map/ppermute | solution.py:21
  3.0 34.7 %all-gather = s32[2,1,8]{2,1,0:T(1,128)S(1)} all-gather(s32[1,1,8]{2,1,0:T(1,128)} %bitcast.117), channel_id=1, replica_groups=mesh['depth'=2,'lat'=8,'freq'=2] {'depth'}, dimensions={0}, use_global_device_ids=true | all-gather | bytes 96 | tf_op jit(solution)/shard_map/all_gather | solution.py:81
  37.7 4.5 %all-gather.1 = f32[2,1,1024]{2,1,0:T(1,128)S(1)} all-gather(f32[1,1,1024]{2,1,0:T(1,128)} %bitcast.116), channel_id=1, replica_groups=mesh['depth'=2,'lat'=8,'freq'=2] {'depth'}, dimensions={0}, use_global_device_ids=true | all-gather | bytes 12288 | tf_op jit(solution)/shard_map/all_gather | solution.py:83
  42.2 1.3 dynamic-slice
  43.5 4.5 %all_gather.12 = s32[2,8,10]{2,1,0:T(8,128)S(1)} all-gather(s32[1,8,10]{2,1,0:T(8,128)} %param.11), channel_id=1, replica_groups=mesh['depth'=2,'lat'=8,'freq'=2] {'depth'}, dimensions={0}, use_global_device_ids=true | all-gather | bytes 960 | tf_op jit(solution)/shard_map/all_gather | solution.py:79
  48.0 4.5 %all_gather.14 = s32[2,8,10]{2,1,0:T(8,128)S(1)} all-gather(s32[1,8,10]{2,1,0:T(8,128)} %param.12), channel_id=1, replica_groups=mesh['depth'=2,'lat'=8,'freq'=2] {'depth'}, dimensions={0}, use_global_device_ids=true | all-gather | bytes 960 | tf_op jit(solution)/shard_map/all_gather | solution.py:80
  52.5 0.0 copy-done
  52.5 1.0 constant_dynamic-slice_fusion.2
  53.5 0.0 collective-permute-done.2
  53.5 1.7 pad_maximum_fusion
  55.2 2.6 %fusion.16 = bf16[2,3,8,128,256]{4,3,2,1,0:T(8,128)(2,1)} fusion(bf16[2,1,1,3,8,128,256]{6,5,4,3,0,2,1:T(8,128)(2,1)S(1)} %pad_maximum_fusion, pred[]{:T(512)S(6)} %eq.11), kind=kLoop, calls=%fused_computation.44 | loop fusion | flops 1572864 | bytes 6291457 | tf_op jit(solution)/shard_map/reshape;reshape | solution.py:13
  57.7 117.8 %while.17 = (s32[]{:T(128)}, bf16[3,2,64,1024]{3,2,1,0:T(8,128)(2,1)}, f32[2,1024]{1,0:T(2,128)S(1)}, s32[2,8,10]{2,1,0:T(8,128)S(1)}, s32[]{:T(128)}, /*index=5...) while((s32[]{:T(128)}, ...), condition=%wide.region_2.3_spmd, body=%wide.region_0.2_spmd.sunk | while | flops 2040010240 | bytes 96773536 | solution.py:101
  57.7 4.8 %collective-permute-start = (bf16[3,2,64,1024]{3,2,1,0:T(8,128)(2,1)}, bf16[3,2,64,1024]{3,2,1,0:T(8,128)(2,1)}, u32[]{:S(2)}, u32[]{:S(2)}) collective-permute-start(bf16[3,2,64,1024]{3,2,1,0:T(8,128)(2,1)} %get-tuple-element.336), channel_id=1, source_target_pairs={{2,0},{4,2},{6,4},{8,6},{10,8},{12,10},{14,12},{0,14},{3,1},{5,3},... | collective-permute-start | bytes 2359304 | tf_op jit(solution)/shard_map/while/body/eval_jaxpr/ppermute | solution.py:37
  62.5 0.0 collective-permute-start.1
  62.5 1.5 dynamic-slice_bitcast_fusion.2
  64.0 0.1 reshape.235
  64.1 0.1 reshape.236
  64.2 8.2 %gather_fusion = bf16[80,3,128,256]{3,2,1,0:T(8,128)(2,1)} fusion(bf16[3,8,128,256]{3,2,1,0:T(8,128)(2,1)S(1)} %dynamic-slice_bitcast_fusion.2, s32[1024]{0:T(1024)S(1)} %pad_clamp_fusion.4), kind=kCustom, calls=%fused_computation.1.clone.1 | custom fusion | bytes 31457600 | tf_op jit(solution)/shard_map/while/body/eval_jaxpr/jit(_take)/gather | solution.py:54
  72.4 0.1 fusion.29
  72.5 17.5 %collective-permute-done = bf16[3,2,64,1024]{3,2,1,0:T(8,128)(2,1)} collective-permute-done((bf16[3,2,64,1024]{3,2,1,0:T(8,128)(2,1)}, bf16[3,2,64,1024]{3,2,1,0:T(8,128)(2,1)}, u32[]{:S(2)}, u32[]{:S(2)}) %collective-permute-start) | collective-permute-done | bytes 786464 | tf_op jit(solution)/shard_map/while/body/eval_jaxpr/ppermute | solution.py:37
  90.0 0.0 collective-permute-done.1
  90.0 3.7 %copy_bitcast_fusion.3 = bf16[3,2,64,24,128]{4,2,3,1,0:T(8,128)(2,1)} fusion(bf16[3,2,64,1024]{3,2,1,0:T(8,128)(2,1)} %collective-permute-done, bf16[3,2,64,1024]{3,2,1,0:T(8,128)(2,1)} %get-tuple-element.336, bf16[3,2,64,1024]{3,2,1,0:T(8,128)(2,1)} %collective-permute-done.1), kind=kLoop, calls=%fused_computation.7.clone.1 | loop fusion | flops 7077888 | bytes 4718592 | tf_op jit(solution)/shard_map/while/body/eval_jaxpr/reshape | solution.py:51
  93.7 8.5 %gather_fusion.1 = bf16[80,3,2,64,128]{4,3,2,1,0:T(8,128)(2,1)} fusion(bf16[3,2,64,24,128]{4,2,3,1,0:T(8,128)(2,1)} %copy_bitcast_fusion.3, s32[1024]{0:T(1024)S(1)} %pad_clamp_fusion.5), kind=kCustom, calls=%fused_computation.clone.1 | custom fusion | bytes 15728960 | tf_op jit(solution)/shard_map/while/body/eval_jaxpr/jit(_take)/gather | solution.py:53
  102.2 10.2 %fusion.30 = f32[8,3,2,64,256]{4,3,2,1,0:T(8,128)S(1)} fusion(bf16[8,10,3,128,256]{4,3,2,1,0:T(8,128)(2,1)} %bitcast.106, pred[8,10]{1,0:T(8,128)(4,1)S(1)} %get-tuple-element.317, bf16[8,10,3,2,64,128]{5,4,3,2,1,0:T(8,128)(2,1)} %bitcast.105, pred[8,10]{1,0:T(8,128)(4,1)S(1)} %get-tuple-element.319, bf16[8,10]{1,0:T(8,128)(2,1)S(1)} %fusion.29), kind=kOutput, calls=%fused_computation.9.clone.1 | convolution fusion | flops 2028994560 | bytes 26739008 | tf_op jit(solution)/shard_map/while/body/eval_jaxpr/fsarkt,frktc->rfsac/dot_general | solution.py:55
  112.5 0.2 slice_subtract_fusion.2
  112.7 0.3 fusion.32
  113.0 1.1 fusion.31
  114.2 4.8 %collective-permute-start = (bf16[3,2,64,1024]{3,2,1,0:T(8,128)(2,1)}, bf16[3,2,64,1024]{3,2,1,0:T(8,128)(2,1)}, u32[]{:S(2)}, u32[]{:S(2)}) collective-permute-start(bf16[3,2,64,1024]{3,2,1,0:T(8,128)(2,1)} %get-tuple-element.336), channel_id=1, source_target_pairs={{2,0},{4,2},{6,4},{8,6},{10,8},{12,10},{14,12},{0,14},{3,1},{5,3},... | collective-permute-start | bytes 2359304 | tf_op jit(solution)/shard_map/while/body/eval_jaxpr/ppermute | solution.py:37
  118.9 0.0 collective-permute-start.1
  118.9 1.5 dynamic-slice_bitcast_fusion.2
  120.5 0.1 reshape.235
  120.6 0.1 reshape.236
  120.7 8.2 %gather_fusion = bf16[80,3,128,256]{3,2,1,0:T(8,128)(2,1)} fusion(bf16[3,8,128,256]{3,2,1,0:T(8,128)(2,1)S(1)} %dynamic-slice_bitcast_fusion.2, s32[1024]{0:T(1024)S(1)} %pad_clamp_fusion.4), kind=kCustom, calls=%fused_computation.1.clone.1 | custom fusion | bytes 31457600 | tf_op jit(solution)/shard_map/while/body/eval_jaxpr/jit(_take)/gather | solution.py:54
  128.9 0.1 fusion.29
  129.0 22.5 %collective-permute-done = bf16[3,2,64,1024]{3,2,1,0:T(8,128)(2,1)} collective-permute-done((bf16[3,2,64,1024]{3,2,1,0:T(8,128)(2,1)}, bf16[3,2,64,1024]{3,2,1,0:T(8,128)(2,1)}, u32[]{:S(2)}, u32[]{:S(2)}) %collective-permute-start) | collective-permute-done | bytes 786464 | tf_op jit(solution)/shard_map/while/body/eval_jaxpr/ppermute | solution.py:37
  151.4 0.0 collective-permute-done.1
  151.4 3.7 %copy_bitcast_fusion.3 = bf16[3,2,64,24,128]{4,2,3,1,0:T(8,128)(2,1)} fusion(bf16[3,2,64,1024]{3,2,1,0:T(8,128)(2,1)} %collective-permute-done, bf16[3,2,64,1024]{3,2,1,0:T(8,128)(2,1)} %get-tuple-element.336, bf16[3,2,64,1024]{3,2,1,0:T(8,128)(2,1)} %collective-permute-done.1), kind=kLoop, calls=%fused_computation.7.clone.1 | loop fusion | flops 7077888 | bytes 4718592 | tf_op jit(solution)/shard_map/while/body/eval_jaxpr/reshape | solution.py:51
  155.1 8.5 %gather_fusion.1 = bf16[80,3,2,64,128]{4,3,2,1,0:T(8,128)(2,1)} fusion(bf16[3,2,64,24,128]{4,2,3,1,0:T(8,128)(2,1)} %copy_bitcast_fusion.3, s32[1024]{0:T(1024)S(1)} %pad_clamp_fusion.5), kind=kCustom, calls=%fused_computation.clone.1 | custom fusion | bytes 15728960 | tf_op jit(solution)/shard_map/while/body/eval_jaxpr/jit(_take)/gather | solution.py:53
  163.6 10.2 %fusion.30 = f32[8,3,2,64,256]{4,3,2,1,0:T(8,128)S(1)} fusion(bf16[8,10,3,128,256]{4,3,2,1,0:T(8,128)(2,1)} %bitcast.106, pred[8,10]{1,0:T(8,128)(4,1)S(1)} %get-tuple-element.317, bf16[8,10,3,2,64,128]{5,4,3,2,1,0:T(8,128)(2,1)} %bitcast.105, pred[8,10]{1,0:T(8,128)(4,1)S(1)} %get-tuple-element.319, bf16[8,10]{1,0:T(8,128)(2,1)S(1)} %fusion.29), kind=kOutput, calls=%fused_computation.9.clone.1 | convolution fusion | flops 2028994560 | bytes 26739008 | tf_op jit(solution)/shard_map/while/body/eval_jaxpr/fsarkt,frktc->rfsac/dot_general | solution.py:55
  173.8 0.2 slice_subtract_fusion.2
  174.1 0.3 fusion.32
  174.4 1.1 fusion.31
  175.6 5.0 %all-reduce = f32[2,1024]{1,0:T(2,128)S(1)} all-reduce(f32[2,1024]{1,0:T(2,128)S(1)} %get-tuple-element.226), channel_id=2, replica_groups=mesh['depth'=2,'lat'=8,'freq'=2] {'depth'}, use_global_device_ids=true, to_apply=%region_3.4.clone | all-reduce | flops 2048 | bytes 16384
  180.6 0.6 constant_dynamic-slice_fusion.1
  181.2 2.5 %psum.7 = f32[1024]{0:T(1024)S(1)} all-reduce(f32[1024]{0:T(1024)S(1)} %bitcast.114), channel_id=1, replica_groups=mesh['depth'=2,'lat'=8,'freq'=2] {'freq'}, use_global_device_ids=true, to_apply=%region_4.5 | all-reduce | flops 1024 | bytes 8192 | tf_op jit(solution)/shard_map/psum | solution.py:103
  183.7 0.6 broadcast_multiply_fusion
  (16 shorter events, 0.2 us)
Async XLA Ops:
  0.0 52.5 %copy-start = (bf16[3,2,128,1024]{3,2,1,0:T(8,128)(2,1)S(1)}, bf16[3,2,128,1024]{3,2,1,0:T(8,128)(2,1)}, u32[]{:S(2)}) copy-start(bf16[3,2,128,1024]{3,2,1,0:T(8,128)(2,1)} %param.8) | copy-start | bytes 4718596
  0.0 53.5 %collective-permute-start.2 = (bf16[1,1,3,8,128,256]{5,4,3,2,1,0:T(8,128)(2,1)}, bf16[1,1,3,8,128,256]{5,4,3,2,1,0:T(8,128)(2,1)S(1)}, u32[]{:S(2)}, u32[]{:S(2)}) collective-permute-start(bf16[1,1,3,8,128,256]{5,4,3,2,1,0:T(8,128)(2,1)} %bitcast.107), channel_id=1, source_target_pairs={{0,16},{16,0},{1,17},{17,1},{2,18},{18,2},{3,19},{19,3},{4,20},{20... | collective-permute-start | bytes 4718600 | tf_op jit(solution)/shard_map/ppermute | solution.py:21
  57.7 32.3 %collective-permute-start = (bf16[3,2,64,1024]{3,2,1,0:T(8,128)(2,1)}, bf16[3,2,64,1024]{3,2,1,0:T(8,128)(2,1)}, u32[]{:S(2)}, u32[]{:S(2)}) collective-permute-start(bf16[3,2,64,1024]{3,2,1,0:T(8,128)(2,1)} %get-tuple-element.336), channel_id=1, source_target_pairs={{2,0},{4,2},{6,4},{8,6},{10,8},{12,10},{14,12},{0,14},{3,1},{5,3},... | collective-permute-start | bytes 2359304 | tf_op jit(solution)/shard_map/while/body/eval_jaxpr/ppermute | solution.py:37
  62.5 27.6 %collective-permute-start.1 = (bf16[3,2,64,1024]{3,2,1,0:T(8,128)(2,1)}, bf16[3,2,64,1024]{3,2,1,0:T(8,128)(2,1)}, u32[]{:S(2)}, u32[]{:S(2)}) collective-permute-start(bf16[3,2,64,1024]{3,2,1,0:T(8,128)(2,1)} %get-tuple-element.336), channel_id=1, source_target_pairs={{0,2},{2,4},{4,6},{6,8},{8,10},{10,12},{12,14},{14,0},{1,3},{3,5},... | collective-permute-start | bytes 2359304 | tf_op jit(solution)/shard_map/while/body/eval_jaxpr/ppermute | solution.py:34
  114.2 37.3 %collective-permute-start = (bf16[3,2,64,1024]{3,2,1,0:T(8,128)(2,1)}, bf16[3,2,64,1024]{3,2,1,0:T(8,128)(2,1)}, u32[]{:S(2)}, u32[]{:S(2)}) collective-permute-start(bf16[3,2,64,1024]{3,2,1,0:T(8,128)(2,1)} %get-tuple-element.336), channel_id=1, source_target_pairs={{2,0},{4,2},{6,4},{8,6},{10,8},{12,10},{14,12},{0,14},{3,1},{5,3},... | collective-permute-start | bytes 2359304 | tf_op jit(solution)/shard_map/while/body/eval_jaxpr/ppermute | solution.py:37
  118.9 32.5 %collective-permute-start.1 = (bf16[3,2,64,1024]{3,2,1,0:T(8,128)(2,1)}, bf16[3,2,64,1024]{3,2,1,0:T(8,128)(2,1)}, u32[]{:S(2)}, u32[]{:S(2)}) collective-permute-start(bf16[3,2,64,1024]{3,2,1,0:T(8,128)(2,1)} %get-tuple-element.336), channel_id=1, source_target_pairs={{0,2},{2,4},{4,6},{6,8},{8,10},{10,12},{12,14},{14,0},{1,3},{3,5},... | collective-permute-start | bytes 2359304 | tf_op jit(solution)/shard_map/while/body/eval_jaxpr/ppermute | solution.py:34
